TPU v7x, 128 devices: a whole 4x4x4 slice. The times are simulated.
128 devices in a mesh: grp: 4 (over x), mem: 32 (over z, y, core).
Axes of the slice: x: 4, y: 4, z: 4, core: 2. Of those that a mesh axis runs over, the one named last changes fastest.
Arguments:
- embeddings: bfloat16 [16384, 1024], P(('grp', 'mem')), may hold values from -6 to 6
- cluster: int32 [16384, 1], P(('grp', 'mem')), may hold values from 0 to 3; in each aligned block of 128 rows (0 to 127, 128 to 255, ...) at most 64 rows name the same one
- rank: int32 [16384], P(('grp', 'mem')), may hold values from 0 to 1048575
Outputs:
- similarity: float32 [16384], P(('grp', 'mem'))
Inputs may be any that keep to these rules, and one draw needn't show every extreme that they name: `cluster`: in each aligned block of 128 rows (the rows of one device) no group is named by more than 64 rows. A smaller rank is earlier; equal ranks are not earlier.
All inputs are finite; a program needn't handle non-finite values.
Results may differ from a plain program's by a relative error of at most 0.0013.
Values may be sent and summed in bfloat16 or wider, within the bound.
A program may use at most 64 MiB of HBM per device.

v0:
```python
import jax
import jax.numpy as jnp
from jax import lax
from jax.sharding import PartitionSpec as P

absent_rank = 1073741824


def block_gram(queries, others):
    return lax.dot_general(
        queries, others, (((1,), (1,)), ((), ())), preferred_element_type=jnp.float32
    )


def row_maxima(gram, query_rank, other_rank):
    earlier = other_rank[None, :] < query_rank[:, None]
    return jnp.max(jnp.where(earlier, gram, jnp.float32(-1.0)), axis=1)


def body(embeddings, cluster, rank):
    rows = embeddings.shape[0]
    width = embeddings.shape[1]
    groups = lax.axis_size("grp")
    capacity = max(2, 2 * rows // groups)
    slots = groups * capacity
    wide = embeddings.astype(jnp.float32)
    normed = (wide * lax.rsqrt(jnp.sum(wide * wide, axis=1, keepdims=True) + 1e-06)).astype(
        jnp.bfloat16
    )
    owner = cluster[:, 0]
    onehot = (owner[:, None] == jnp.arange(groups, dtype=jnp.int32)[None, :]).astype(jnp.int32)
    before = jnp.cumsum(onehot, axis=0) - onehot
    position = jnp.sum(before * onehot, axis=1)
    slot = owner * capacity + position
    outgoing = jnp.zeros((slots, width), jnp.bfloat16).at[slot].set(normed)
    out_rank = jnp.full((slots,), absent_rank, jnp.int32).at[slot].set(rank)
    keys, key_rank = (
        lax.all_to_all(outgoing, "grp", split_axis=0, concat_axis=0, tiled=True),
        lax.all_to_all(out_rank, "grp", split_axis=0, concat_axis=0, tiled=True),
    )
    gram = block_gram(keys, lax.all_gather(keys, "mem", axis=0, tiled=True))
    best = jnp.maximum(
        jnp.full((slots,), -1.0, jnp.float32),
        row_maxima(gram, key_rank, lax.all_gather(key_rank, "mem", axis=0, tiled=True)),
    )
    home = lax.all_to_all(best, "grp", split_axis=0, concat_axis=0, tiled=True)
    return home[slot]


def solution(mesh):
    in_specs = (P(("grp", "mem"), None), P(("grp", "mem"), None), P(("grp", "mem")))
    out_specs = P(("grp", "mem"))
    return jax.shard_map(body, mesh=mesh, in_specs=in_specs, out_specs=out_specs, check_vma=False)
```

profile of v0, /device:TPU:1, one launch (start us, length us, event | category | flops | bytes accessed | tf_op | source)
XLA Modules:
  0.0 129.4 jit_solution(2143554724468487378)
XLA Ops:
  6.5 0.0 all-gather.3.cloned.1.call-start
  6.5 0.7 fusion.7
  7.3 0.2 reduce_window_sum.11
  7.5 0.8 select_reduce_fusion
  8.3 0.7 fusion.8
  9.0 1.1 fusion.1
  10.0 1.8 %scatter_custom_fusion.1 = bf16[256,1024]{1,0:T(8,128)(2,1)S(1)} fusion(s32[128]{0:T(128)S(1)} %fusion.8, bf16[128,1024]{1,0:T(8,128)(2,1)} %param.3, f32[128]{0:T(128)S(1)} %add_rsqrt_fusion, bf16[]{:T(256)} %constant.4.clone.1), kind=kCustom, calls=%fused_computation.9 | custom fusion | flops 393216 | bytes 786946 | tf_op jit(solution)/shard_map/scatter | solution.py:35
  11.8 13.4 %all_to_all.33 = bf16[4,64,1024]{2,1,0:T(8,128)(2,1)} all-to-all(bf16[4,64,1024]{2,1,0:T(8,128)(2,1)S(1)} %bitcast.19), channel_id=1, replica_groups=mesh['grp'=4,'mem'=32] {'grp'}, dimensions={0} | all-to-all | bytes 1048576 | tf_op jit(solution)/shard_map/all_to_all | solution.py:38
  25.2 0.0 all-gather.3.cloned.1.call-update
  25.2 1.1 scatter_custom_fusion
  26.3 0.1 all_to_all.22
  26.4 6.5 %all_to_all.34 = s32[4,64,1]{1,2,0:T(1,128)S(1)} all-to-all(s32[4,64,1]{1,2,0:T(1,128)S(1)} %bitcast.22), channel_id=1, replica_groups=mesh['grp'=4,'mem'=32] {'grp'}, dimensions={0} | all-to-all | bytes 2048 | tf_op jit(solution)/shard_map/all_to_all | solution.py:39
  32.9 0.1 all_to_all.24
  33.0 0.5 broadcast.45
  33.5 0.7 reduce.8
  34.1 0.1 reshape.52
  34.2 28.6 %all-gather = s32[32,1,256]{2,1,0:T(1,128)S(1)} all-gather(s32[1,1,256]{2,1,0:T(1,128)S(1)} %reshape.52), channel_id=1, replica_groups=mesh['grp'=4,'mem'=32] {'mem'}, dimensions={0}, use_global_device_ids=true | all-gather | bytes 33792 | tf_op jit(solution)/shard_map/all_gather | solution.py:44
  62.9 37.3 %all-gather.3.cloned.1.call-done = bf16[8192,1024]{1,0:T(8,128)(2,1)} async-done(((bf16[256,1024]{1,0:T(8,128)(2,1)}), bf16[8192,1024]{1,0:T(8,128)(2,1)}) %all-gather.3.cloned.1.call-update) | async-done | bytes 16777232 | tf_op jit(solution)/shard_map/all_gather | solution.py:41
  100.2 10.6 %fusion = f32[256]{0:T(256)S(1)} fusion(bf16[256,1024]{1,0:T(8,128)(2,1)} %bitcast.18, bf16[8192,1024]{1,0:T(8,128)(2,1)} %all-gather.3.cloned.1.call-done, s32[256]{0:T(256)S(1)} %all_to_all.24, s32[8192]{0:T(1024)S(1)} %bitcast.20), kind=kOutput, calls=%fused_computation.4 | convolution fusion | flops 4301258752 | bytes 17336320 | tf_op jit(solution)/shard_map/dot_general | solution.py:10
  110.8 0.7 max_broadcast_in_dim.14
  111.5 4.0 %all-to-all-start.2 = ((f32[4,64,1]{1,2,0:T(1,128)}), f32[4,64,1]{1,2,0:T(1,128)S(1)}, u32[]{:S(2)}, u32[]{:S(2)}) async-start(f32[4,64,1]{1,2,0:T(1,128)} %bitcast.7), calls=%async_computation.2 | async-start | bytes 4096 | tf_op jit(solution)/shard_map/all_to_all | solution.py:46
  115.4 4.1 %all-to-all-done.2 = f32[4,64,1]{1,2,0:T(1,128)S(1)} async-done(((f32[4,64,1]{1,2,0:T(1,128)}), f32[4,64,1]{1,2,0:T(1,128)S(1)}, u32[]{:S(2)}, u32[]{:S(2)}) %all-to-all-start.2) | async-done | bytes 1056 | tf_op jit(solution)/shard_map/all_to_all | solution.py:46
  119.6 0.5 broadcast.46
  120.1 0.7 reduce.9
  120.7 0.1 all_to_all.29
  120.8 1.8 %gather_fusion = f32[128]{0:T(128)} fusion(f32[256]{0:T(256)S(1)} %all_to_all.29, s32[1024]{0:T(1024)S(1)} %pad_clamp_fusion), kind=kCustom, calls=%fused_computation | custom fusion | bytes 1536 | tf_op jit(solution)/shard_map/gather | solution.py:47
  (3 shorter events, 0.0 us)
Async XLA Ops:
  6.5 93.6 %all-gather.3.cloned.1.call-start = ((), (), s32[]{:S(2)}) async-start(), calls=%async_computation.3 | async-start | bytes 17301504 | tf_op jit(solution)/shard_map/all_gather | solution.py:41
  111.5 8.1 %all-to-all-start.2 = ((f32[4,64,1]{1,2,0:T(1,128)}), f32[4,64,1]{1,2,0:T(1,128)S(1)}, u32[]{:S(2)}, u32[]{:S(2)}) async-start(f32[4,64,1]{1,2,0:T(1,128)} %bitcast.7), calls=%async_computation.2 | async-start | bytes 4096 | tf_op jit(solution)/shard_map/all_to_all | solution.py:46
Sparse Core Ops, SparseCore 0:
  25.3 74.7 all-gather.2
where the time goes:
time: 130 us; the launch traced here: 129 us
  blocking collectives  48.5 us (37%)
  waiting for transfers between devices  41.4 us (32%)
  between operations  13.4 us (10%)
  matrix products  10.6 us (8%)
  other arithmetic  6.62 us (5%)
  local copies, waits for them, and re-layouts  4.9 us (4%)
  starting transfers between devices  3.97 us (3%)
    all_gather x1, waiting for transfers between devices, body(): gram = block_gram(keys, lax.all_gather(keys, 'mem', axis=0, tiled=True))  37.3 us
    all_gather x1, blocking collectives, body(): lax.all_gather(key_rank, 'mem', axis=0, tiled=True)  28.6 us
    all_to_all x1, blocking collectives, body(): lax.all_to_all(outgoing, 'grp', split_axis=0, concat_axis=0, tiled=True)  13.4 us
    dot_general x1, matrix products, block_gram(): lax.dot_general(queries, others, (((1,), (1,)), ((), ())), preferred_elem...  10.6 us
    all_to_all x1, blocking collectives, body(): lax.all_to_all(out_rank, 'grp', split_axis=0, concat_axis=0, tiled=True)  6.46 us
    all_to_all x1, waiting for transfers between devices, body(): home = lax.all_to_all(best, 'grp', split_axis=0, concat_axis=0, tiled=True)  4.13 us
    all_to_all x1, starting transfers between devices, body(): home = lax.all_to_all(best, 'grp', split_axis=0, concat_axis=0, tiled=True)  3.97 us
  transfers between devices with their start and end apart: 2, of which 2 were waited for; matrix products, arithmetic and copies ran while one was open for 2% of the time, Pallas kernels for 0%

commit v1 on v0

v1 whole, which is shorter than its diff:
```python
import jax
import jax.numpy as jnp
from jax import lax
from jax.experimental import pallas as pl
from jax.experimental.pallas import tpu as pltpu
from jax.sharding import PartitionSpec as P

MESH = pl.DeviceIdType.MESH
OFFSETS = (
    (0, 0, 0), (0, 0, 1), (0, 0, 2), (0, 0, 3), (0, 1, 0), (0, 2, 0), (1, 0, 0),
    (1, 1, 0), (1, 2, 0), (1, 3, 0), (3, 0, 0), (3, 0, 1), (3, 0, 2),
)
UNITS = ((1, 0, 0), (3, 0, 0), (0, 1, 0), (0, 3, 0), (0, 0, 1), (0, 0, 3))
PIECES = 4
PROGRAM = (
    ("s", 1, 2, 0, 4), ("s", 3, 0, 0, 5), ("s", 4, 0, 0, 2), ("s", 6, 1, 0, 0), ("s", 10, 0, 0, 1),
    ("x", 0), ("s", 1, 3, 0, 4), ("s", 3, 1, 0, 5), ("s", 4, 2, 0, 2), ("s", 6, 3, 0, 0),
    ("s", 10, 1, 0, 1), ("u", 0, 0), ("s", 1, 0, 0, 4), ("s", 3, 2, 0, 5), ("s", 4, 1, 0, 2),
    ("s", 6, 0, 0, 0), ("s", 10, 2, 0, 1), ("s", 9, 1, 6, 3), ("s", 2, 0, 3, 5), ("s", 4, 3, 0, 2),
    ("s", 7, 0, 4, 0), ("s", 11, 0, 10, 4), ("s", 11, 2, 1, 1), ("s", 9, 3, 6, 3), ("s", 1, 1, 0, 4),
    ("s", 2, 1, 3, 5), ("s", 5, 2, 4, 2), ("s", 6, 2, 0, 0), ("s", 11, 3, 1, 1), ("s", 9, 0, 6, 3),
    ("s", 3, 3, 0, 5), ("s", 5, 0, 4, 2), ("s", 7, 1, 4, 0), ("s", 10, 3, 0, 1), ("s", 11, 1, 10, 4),
    ("s", 8, 1, 9, 3), ("x", 4), ("u", 4, 0), ("s", 2, 2, 3, 5), ("s", 7, 2, 4, 0),
    ("s", 8, 0, 7, 2), ("s", 12, 0, 2, 1), ("s", 12, 2, 11, 4), ("s", 9, 2, 6, 3), ("x", 1),
    ("x", 6), ("u", 1, 0), ("u", 6, 0), ("s", 5, 1, 4, 2), ("s", 8, 2, 5, 0),
    ("s", 12, 1, 2, 1), ("s", 12, 3, 11, 4), ("u", 1, 4), ("u", 6, 4), ("s", 2, 3, 3, 5),
    ("s", 8, 3, 9, 3), ("x", 3), ("x", 10), ("x", 11), ("u", 3, 4),
    ("u", 10, 4), ("u", 11, 0), ("s", 5, 3, 4, 2), ("s", 7, 3, 4, 0), ("u", 11, 4),
    ("u", 3, 1), ("u", 3, 6), ("u", 10, 6), ("u", 11, 6), ("x", 9),
    ("u", 9, 1), ("u", 9, 4), ("u", 3, 11), ("x", 12), ("u", 9, 3),
    ("u", 9, 10), ("x", 2), ("u", 9, 11), ("u", 12, 4), ("u", 12, 6),
    ("u", 2, 4), ("u", 8, 1), ("u", 8, 3), ("u", 8, 6), ("u", 8, 10),
    ("u", 8, 11), ("u", 2, 9), ("u", 12, 9), ("u", 5, 1), ("u", 7, 3),
    ("u", 7, 11), ("u", 5, 12), ("u", 8, 12), ("u", 5, 2),
)
HALF = 128
WIDTH = 1024
RANKS = 1048576


def schedule():
    steps = list(PROGRAM)
    last = {}
    shared = sorted({s[1] for s in steps if s[0] == "x"})
    for i, step in enumerate(steps):
        if step[0] == "u":
            last[("own", step[1])] = i
            for which in ("own", "other"):
                last[(which, step[2])] = i
    return steps, shared, last


def kernel(
    x_hbm, cluster_ref, rank_ref, out_ref, raw, blocks, keys, key_columns, row_best, column_best,
    results, returned, raw_sem, send, receive, key_send, key_receive, pair_send, pair_receive,
    pair_key_send, pair_key_receive, back_send, back_receive,
):
    x = lax.axis_index("grp")
    m = lax.axis_index("mem")
    z, y, core = m // 8, (m // 2) % 4, m % 2
    count = len(OFFSETS)
    rows = HALF // PIECES

    def at(offset, which):
        dx, dy, dz = offset
        chip = ((z + dz) % 4) * 8 + ((y + dy) % 4) * 2
        return ((x + dx) % 4, chip + which)

    barrier = pltpu.get_barrier_semaphore()
    for unit in UNITS:
        pl.semaphore_signal(barrier, inc=1, device_id=at(unit, core), device_id_type=MESH)
    pl.semaphore_signal(
        barrier, inc=1, device_id=at((0, 0, 0), 1 - core), device_id_type=MESH
    )
    load = pltpu.make_async_copy(x_hbm, raw, raw_sem)
    load.start()
    keys[0, core] = cluster_ref[...] * (2 * RANKS) + rank_ref[...]
    row_best[...] = jnp.full(row_best.shape, -1.0, jnp.float32)
    column_best[...] = jnp.full(column_best.shape, -1.0, jnp.float32)
    load.wait()
    wide = raw[...].astype(jnp.float32)
    scale = lax.rsqrt(jnp.sum(wide * wide, axis=1, keepdims=True) + 1e-06)
    blocks[0, core] = (wide * scale).astype(jnp.bfloat16)
    pl.semaphore_wait(barrier, 7)

    steps, shared, last = schedule()
    sent = []
    arrived = set((0, piece) for piece in range(PIECES))
    key_here = {0}
    pair_here = set()
    columns_here = set()

    def copy(source, target, send_sem, receive_sem, device):
        return pltpu.make_async_remote_copy(
            src_ref=source, dst_ref=target, send_sem=send_sem, recv_sem=receive_sem,
            device_id=device, device_id_type=MESH,
        )

    def piece_copy(slot, piece, parent, direction):
        back = UNITS[direction ^ 1]
        part = pl.ds(piece * rows, rows)
        return copy(
            blocks.at[parent, core, part], blocks.at[slot, core, part],
            send.at[slot, piece], receive.at[slot, piece], at(back, core),
        )

    def key_copy(slot, parent, direction):
        back = UNITS[direction ^ 1]
        return copy(
            keys.at[parent, core], keys.at[slot, core],
            key_send.at[slot], key_receive.at[slot], at(back, core),
        )

    def pair_copy(slot):
        return copy(
            blocks.at[slot, core], blocks.at[slot, core],
            pair_send.at[slot], pair_receive.at[slot], at((0, 0, 0), 1 - core),
        )

    def pair_key_copy(slot):
        return copy(
            keys.at[slot, core], keys.at[slot, core],
            pair_key_send.at[slot], pair_key_receive.at[slot], at((0, 0, 0), 1 - core),
        )

    incoming = {(s[1], s[2]): s[1:] for s in steps if s[0] == "s"}

    def need_piece(slot, piece):
        if (slot, piece) not in arrived:
            piece_copy(*incoming[(slot, piece)]).wait_recv()
            arrived.add((slot, piece))

    def need_key(slot):
        if slot not in key_here:
            _, _, parent, direction = incoming[(slot, 0)]
            key_copy(slot, parent, direction).wait_recv()
            key_here.add(slot)

    def need_block(slot):
        for piece in range(PIECES):
            need_piece(slot, piece)
        need_key(slot)

    def need_pair(slot):
        if slot not in pair_here:
            copy(
                blocks.at[slot, 1 - core], blocks.at[slot, 1 - core],
                pair_send.at[slot], pair_receive.at[slot], at((0, 0, 0), 1 - core),
            ).wait_recv()
            copy(
                keys.at[slot, 1 - core], keys.at[slot, 1 - core],
                pair_key_send.at[slot], pair_key_receive.at[slot], at((0, 0, 0), 1 - core),
            ).wait_recv()
            pair_here.add(slot)

    def need_columns(slot):
        if slot not in columns_here:
            key_columns[slot] = jnp.broadcast_to(keys[slot, core], (HALF, HALF)).T
            columns_here.add(slot)

    def multiply(a, b):
        need_block(a)
        need_block(b)
        need_pair(b)
        need_columns(a)
        gram = lax.dot_general(
            blocks[a, core], blocks[b].reshape(2 * HALF, WIDTH), (((1,), (1,)), ((), ())),
            preferred_element_type=jnp.float32,
        )
        best = row_best[a]
        for half in range(2):
            part = gram[:, half * HALF : (half + 1) * HALF]
            gap = key_columns[a] - keys[b, half]
            part = jnp.where(jnp.abs(gap) < RANKS, part, -1.0)
            best = jnp.maximum(best, jnp.where(gap > 0, part, -1.0))
            lower = jnp.where(gap < 0, part, -1.0).reshape(HALF // 8, 8, HALF)
            column_best[b, half] = jnp.maximum(column_best[b, half], jnp.max(lower, axis=0))
        row_best[a] = best

    ready = []

    def back_copy(which, slot):
        place = slot if which == "own" else count + slot
        device = at(OFFSETS[slot], core if which == "own" else 1 - core)
        return copy(
            results.at[place], returned.at[place],
            back_send.at[place], back_receive.at[place], device,
        )

    def finish(which, slot):
        place = slot if which == "own" else count + slot
        if which == "own":
            value = jnp.max(row_best[slot].T, axis=0, keepdims=True)
            if slot in shared:
                value = jnp.maximum(
                    value, jnp.max(column_best[slot, core], axis=0, keepdims=True)
                )
        else:
            value = jnp.max(column_best[slot, 1 - core], axis=0, keepdims=True)
        results[place] = value

    def send_back():
        for which, slot in ready:
            if (which, slot) != ("own", 0):
                c = back_copy(which, slot)
                c.start()
                sent.append(c)
        ready.clear()

    for i, step in enumerate(steps):
        if step[0] == "s":
            _, slot, piece, parent, direction = step
            need_piece(parent, piece)
            c = piece_copy(slot, piece, parent, direction)
            c.start()
            sent.append(c)
            if piece == 0:
                need_key(parent)
                c = key_copy(slot, parent, direction)
                c.start()
                sent.append(c)
        elif step[0] == "x":
            need_block(step[1])
            for c in (pair_copy(step[1]), pair_key_copy(step[1])):
                c.start()
                sent.append(c)
        else:
            multiply(step[1], step[2])
            send_back()
            for which, slot in sorted(k for k, v in last.items() if v == i):
                finish(which, slot)
                ready.append((which, slot))
    send_back()

    total = results[0]
    for which, slot in last:
        if (which, slot) != ("own", 0):
            back_copy(which, slot).wait_recv()
            place = slot if which == "own" else count + slot
            total = jnp.maximum(total, returned[place])
    out_ref[...] = total
    for c in sent:
        c.wait_send()


def body(embeddings, cluster, rank):
    count = len(OFFSETS)
    dma = pltpu.SemaphoreType.DMA
    vmem = pl.BlockSpec(memory_space=pltpu.VMEM)
    found = pl.pallas_call(
        kernel,
        out_shape=jax.ShapeDtypeStruct((1, HALF), jnp.float32),
        in_specs=[pl.BlockSpec(memory_space=pl.ANY), vmem, vmem],
        out_specs=vmem,
        scratch_shapes=[
            pltpu.VMEM((HALF, WIDTH), jnp.bfloat16),
            pltpu.VMEM((count, 2, HALF, WIDTH), jnp.bfloat16),
            pltpu.VMEM((count, 2, 1, HALF), jnp.int32),
            pltpu.VMEM((count, HALF, HALF), jnp.int32),
            pltpu.VMEM((count, HALF, HALF), jnp.float32),
            pltpu.VMEM((count, 2, 8, HALF), jnp.float32),
            pltpu.VMEM((2 * count, 1, HALF), jnp.float32),
            pltpu.VMEM((2 * count, 1, HALF), jnp.float32),
            dma(()),
            dma((count, PIECES)),
            dma((count, PIECES)),
            dma((count,)),
            dma((count,)),
            dma((count,)),
            dma((count,)),
            dma((count,)),
            dma((count,)),
            dma((2 * count,)),
            dma((2 * count,)),
        ],
        compiler_params=pltpu.CompilerParams(collective_id=0, has_side_effects=True),
        name="pairs",
    )(embeddings, cluster.reshape(1, HALF), rank.reshape(1, HALF))
    return found.reshape(HALF)


def solution(mesh):
    in_specs = (P(("grp", "mem"), None), P(("grp", "mem"), None), P(("grp", "mem")))
    out_specs = P(("grp", "mem"))
    return jax.shard_map(body, mesh=mesh, in_specs=in_specs, out_specs=out_specs, check_vma=False)
```

time: 130 us -> 37.2 us (0.29)
  blocking collectives: 48.5 us -> 0 us
  waiting for transfers between devices: 41.4 us -> 0 us
  Pallas kernels: 0 us -> 35.4 us
  between operations: 13.4 us -> 0.02 us
  matrix products: 10.6 us -> 0 us
  other arithmetic: 6.62 us -> 0 us
  starting transfers between devices: 3.97 us -> 0 us
  local copies, waits for them, and re-layouts: 4.9 us -> 1.1 us
    all_gather x1 -> x0, waiting for transfers between devices: 37.3 us -> none  [body(): gram = block_gram(keys, lax.all_gather(keys, 'mem', axis=0, tiled=True))]
    pallas_call x0 -> x1, Pallas kernels: none -> 35.4 us  [body(): pl.pallas_call(kernel, out_shape=jax.ShapeDtypeStruct((1, HALF), jnp.floa...]
    all_gather x1 -> x0, blocking collectives: 28.6 us -> none  [body(): lax.all_gather(key_rank, 'mem', axis=0, tiled=True)]
    all_to_all x2 -> x0, blocking collectives: 19.8 us -> none  [the longest x1 13.4 us: body(): lax.all_to_all(outgoing, 'grp', split_axis=0, concat_axis=0, tiled=True)]
    dot_general x1 -> x0, matrix products: 10.6 us -> none  [block_gram(): lax.dot_general(queries, others, (((1,), (1,)), ((), ())), preferred_elem...]
    all_to_all x1 -> x0, waiting for transfers between devices: 4.13 us -> none  [body(): home = lax.all_to_all(best, 'grp', split_axis=0, concat_axis=0, tiled=True)]
    all_to_all x1 -> x0, starting transfers between devices: 3.97 us -> none  [body(): home = lax.all_to_all(best, 'grp', split_axis=0, concat_axis=0, tiled=True)]
    reduce_sum x2 -> x0, other arithmetic: 1.91 us -> none  [the longest x1 1.08 us: body(): jnp.sum(wide * wide, axis=1, keepdims=True) + 1e-06]
  transfers between devices with their start and end apart: 2 -> 0, of which waited for: 2 -> 0; matrix products, arithmetic and copies ran while one was open for 2% -> 0% of each run, Pallas kernels for 0% -> 0%
where the time goes in v1:
time: 37.2 us; the launch traced here: 36.5 us
  Pallas kernels  35.4 us (95%)
  local copies, waits for them, and re-layouts  1.1 us (3%)
    pallas_call x1, Pallas kernels, body(): pl.pallas_call(kernel, out_shape=jax.ShapeDtypeStruct((1, HALF), jnp.floa...  35.4 us
    unnamed x3, local copies, waits for them, and re-layouts  1.1 us

profile of v1, /device:TPU:1, one launch (start us, length us, event | category | flops | bytes accessed | tf_op | source)
XLA Modules:
  0.0 36.5 jit_solution(8644076877075721771)
XLA Ops:
  0.0 35.4 %pairs.1 = f32[1,128]{1,0:T(1,128)} custom-call(bf16[128,1024]{1,0:T(8,128)(2,1)} %x_hbm.1, s32[1,128]{1,0:T(1,128)} %bitcast.3, s32[1,128]{1,0:T(1,128)} %bitcast.4), custom_call_target="tpu_custom_call" | custom-call | tf_op jit(solution)/shard_map/pairs/pallas_call | solution.py:250
  35.4 0.0 copy-start
  35.4 0.6 %copy-done = f32[1,128]{1,0:T(1,128)S(1)} copy-done((f32[1,128]{1,0:T(1,128)S(1)}, f32[1,128]{1,0:T(1,128)}, u32[]{:S(2)}) %copy-start) | copy-done | bytes 536
  36.0 0.5 %copy.5 = f32[128]{0:T(128)} copy(f32[128]{0:T(128)S(1)} %bitcast.5) | data formatting | bytes 1024
Async XLA Ops:
  35.4 0.6 %copy-start = (f32[1,128]{1,0:T(1,128)S(1)}, f32[1,128]{1,0:T(1,128)}, u32[]{:S(2)}) copy-start(f32[1,128]{1,0:T(1,128)} %pairs.1) | copy-start | bytes 1540

commit v2 on v1

v2 whole, which is shorter than its diff:
```python
import jax
import jax.numpy as jnp
from jax import lax
from jax.experimental import pallas as pl
from jax.experimental.pallas import tpu as pltpu
from jax.sharding import PartitionSpec as P

MESH = pl.DeviceIdType.MESH
OFFSETS = (
    (0, 0, 0), (0, 0, 1), (0, 0, 2), (0, 0, 3), (0, 1, 0), (0, 3, 0), (0, 3, 1),
    (0, 3, 2), (1, 1, 0), (2, 0, 0), (2, 1, 0), (3, 0, 0), (3, 1, 0),
)
UNITS = ((1, 0, 0), (3, 0, 0), (0, 1, 0), (0, 3, 0), (0, 0, 1), (0, 0, 3))
PIECES = 4
PROGRAM = (
    ("s", 11, 3, 0, 1), ("s", 4, 1, 0, 2), ("s", 5, 0, 0, 3), ("s", 1, 1, 0, 4), ("s", 3, 2, 0, 5),
    ("x", 0), ("s", 11, 2, 0, 1), ("s", 4, 2, 0, 2), ("s", 5, 1, 0, 3), ("s", 1, 0, 0, 4),
    ("s", 3, 3, 0, 5), ("s", 11, 1, 0, 1), ("s", 4, 0, 0, 2), ("s", 5, 2, 0, 3), ("s", 1, 3, 0, 4),
    ("s", 3, 0, 0, 5), ("s", 8, 1, 4, 0), ("s", 11, 0, 0, 1), ("s", 12, 3, 11, 2), ("s", 6, 1, 1, 3),
    ("s", 1, 2, 0, 4), ("s", 2, 2, 3, 5), ("s", 8, 2, 4, 0), ("s", 9, 3, 11, 1), ("s", 12, 2, 11, 2),
    ("s", 5, 3, 0, 3), ("s", 6, 0, 5, 4), ("s", 2, 3, 3, 5), ("s", 8, 0, 4, 0), ("s", 12, 1, 4, 1),
    ("s", 4, 3, 0, 2), ("s", 6, 3, 1, 3), ("s", 6, 2, 5, 4), ("s", 3, 1, 0, 5), ("s", 10, 1, 8, 0),
    ("x", 1), ("x", 11), ("s", 9, 0, 11, 1), ("s", 12, 0, 11, 2), ("s", 7, 2, 2, 3),
    ("s", 7, 1, 6, 4), ("s", 2, 0, 3, 5), ("x", 5), ("s", 10, 0, 8, 0), ("u", 1, 0, 1, 5),
    ("s", 10, 2, 12, 1), ("s", 10, 3, 9, 2), ("s", 7, 3, 2, 3), ("s", 7, 0, 6, 4), ("u", 11, 0, 1, 5),
    ("s", 2, 1, 3, 5), ("x", 3), ("x", 4), ("x", 6), ("u", 1, 6, 3, 4),
    ("u", 11, 4), ("s", 8, 3, 4, 0), ("s", 9, 1, 11, 1), ("u", 5, 4), ("x", 12),
    ("u", 1, 12), ("u", 5, 12), ("u", 6, 3, 4, 12), ("s", 9, 2, 11, 1), ("u", 3, 12, 11),
    ("x", 10), ("u", 4, 7, 10), ("u", 11, 7), ("u", 0, 10), ("x", 2),
    ("u", 1, 10), ("u", 3, 10), ("u", 5, 10), ("u", 6, 10, 8), ("u", 12, 7),
    ("u", 10, 2, 7), ("u", 11, 2), ("u", 1, 8, 9), ("u", 3, 8), ("u", 2, 8, 9),
)
HALF = 128
WIDTH = 1024
RANKS = 1048576


def schedule():
    steps = list(PROGRAM)
    last = {}
    shared = sorted({s[1] for s in steps if s[0] == "x"})
    for i, step in enumerate(steps):
        if step[0] == "u":
            for a in step[2:]:
                last[("own", a)] = i
            for which in ("own", "other"):
                last[(which, step[1])] = i
    return steps, shared, last


def kernel(
    x_hbm, cluster_ref, rank_ref, out_ref, raw, blocks, keys, key_columns, row_best, column_best,
    results, returned, raw_sem, send, receive, key_send, key_receive, pair_send, pair_receive,
    pair_key_send, pair_key_receive, back_send, back_receive,
):
    x = lax.axis_index("grp")
    m = lax.axis_index("mem")
    z, y, core = m // 8, (m // 2) % 4, m % 2
    count = len(OFFSETS)
    rows = HALF // PIECES

    def at(offset, which):
        dx, dy, dz = offset
        chip = ((z + dz) % 4) * 8 + ((y + dy) % 4) * 2
        return ((x + dx) % 4, chip + which)

    barrier = pltpu.get_barrier_semaphore()
    for unit in UNITS:
        pl.semaphore_signal(barrier, inc=1, device_id=at(unit, core), device_id_type=MESH)
    pl.semaphore_signal(
        barrier, inc=1, device_id=at((0, 0, 0), 1 - core), device_id_type=MESH
    )
    load = pltpu.make_async_copy(x_hbm, raw, raw_sem)
    load.start()
    keys[0, core] = cluster_ref[...] * (2 * RANKS) + rank_ref[...]
    row_best[...] = jnp.full(row_best.shape, -1.0, jnp.float32)
    column_best[...] = jnp.full(column_best.shape, -1.0, jnp.float32)
    load.wait()
    wide = raw[...].astype(jnp.float32)
    scale = lax.rsqrt(jnp.sum(wide * wide, axis=1, keepdims=True) + 1e-06)
    blocks[0, core] = (wide * scale).astype(jnp.bfloat16)
    pl.semaphore_wait(barrier, 7)

    steps, shared, last = schedule()
    back_place = {k: i for i, k in enumerate(k for k in sorted(last) if k != ("own", 0))}
    arrived = set((0, piece) for piece in range(PIECES))
    key_here = {0}
    pair_here = set()
    columns_here = set()

    def copy(source, target, send_sem, receive_sem, device):
        return pltpu.make_async_remote_copy(
            src_ref=source, dst_ref=target, send_sem=send_sem, recv_sem=receive_sem,
            device_id=device, device_id_type=MESH,
        )

    def piece_copy(slot, piece, parent, direction):
        back = UNITS[direction ^ 1]
        part = pl.ds(piece * rows, rows)
        return copy(
            blocks.at[parent, core, part], blocks.at[slot, core, part],
            send, receive.at[slot, piece], at(back, core),
        )

    def key_copy(slot, parent, direction):
        back = UNITS[direction ^ 1]
        return copy(
            keys.at[parent, core], keys.at[slot, core],
            key_send, key_receive.at[slot], at(back, core),
        )

    def pair_copy(slot):
        return copy(
            blocks.at[slot, core], blocks.at[slot, core],
            pair_send, pair_receive.at[slot], at((0, 0, 0), 1 - core),
        )

    def pair_key_copy(slot):
        return copy(
            keys.at[slot, core], keys.at[slot, core],
            pair_key_send, pair_key_receive.at[slot], at((0, 0, 0), 1 - core),
        )

    incoming = {(s[1], s[2]): s[1:] for s in steps if s[0] == "s"}

    def need_piece(slot, piece):
        if (slot, piece) not in arrived:
            piece_copy(*incoming[(slot, piece)]).wait_recv()
            arrived.add((slot, piece))

    def need_key(slot):
        if slot not in key_here:
            _, _, parent, direction = incoming[(slot, 0)]
            key_copy(slot, parent, direction).wait_recv()
            key_here.add(slot)

    def need_block(slot):
        for piece in range(PIECES):
            need_piece(slot, piece)
        need_key(slot)

    def need_pair(slot):
        if slot not in pair_here:
            copy(
                blocks.at[slot, 1 - core], blocks.at[slot, 1 - core],
                pair_send, pair_receive.at[slot], at((0, 0, 0), 1 - core),
            ).wait_recv()
            copy(
                keys.at[slot, 1 - core], keys.at[slot, 1 - core],
                pair_key_send, pair_key_receive.at[slot], at((0, 0, 0), 1 - core),
            ).wait_recv()
            pair_here.add(slot)

    def need_columns(slot):
        if slot not in columns_here:
            key_columns[slot] = jnp.broadcast_to(keys[slot, core], (HALF, HALF)).T
            columns_here.add(slot)

    def multiply(b, others):
        for a in others:
            need_block(a)
        need_block(b)
        need_pair(b)
        for a in others:
            need_columns(a)
        gram = lax.dot_general(
            jnp.concatenate([blocks[a, core] for a in others], axis=0),
            blocks[b].reshape(2 * HALF, WIDTH), (((1,), (1,)), ((), ())),
            preferred_element_type=jnp.float32,
        )
        for i, a in enumerate(others):
            best = row_best[a]
            for half in range(2):
                part = gram[i * HALF : (i + 1) * HALF, half * HALF : (half + 1) * HALF]
                gap = key_columns[a] - keys[b, half]
                part = jnp.where(jnp.abs(gap) < RANKS, part, -1.0)
                best = jnp.maximum(best, jnp.where(gap > 0, part, -1.0))
                lower = jnp.where(gap < 0, part, -1.0).reshape(HALF // 8, 8, HALF)
                column_best[b, half] = jnp.maximum(column_best[b, half], jnp.max(lower, axis=0))
            row_best[a] = best

    ready = []

    def back_copy(which, slot):
        place = back_place[(which, slot)]
        device = at(OFFSETS[slot], core if which == "own" else 1 - core)
        return copy(
            results.at[place], returned.at[place],
            back_send, back_receive, device,
        )

    def finish(which, slot):
        if which == "own":
            value = jnp.max(row_best[slot].T, axis=0, keepdims=True)
            if slot in shared:
                value = jnp.maximum(
                    value, jnp.max(column_best[slot, core], axis=0, keepdims=True)
                )
        else:
            value = jnp.max(column_best[slot, 1 - core], axis=0, keepdims=True)
        results[back_place.get((which, slot), len(back_place))] = value

    def send_back():
        for which, slot in ready:
            if (which, slot) != ("own", 0):
                c = back_copy(which, slot)
                c.start()
        ready.clear()

    for i, step in enumerate(steps):
        if step[0] == "s":
            _, slot, piece, parent, direction = step
            need_piece(parent, piece)
            c = piece_copy(slot, piece, parent, direction)
            c.start()
            if piece == 0:
                need_key(parent)
                c = key_copy(slot, parent, direction)
                c.start()
        elif step[0] == "x":
            need_block(step[1])
            for c in (pair_copy(step[1]), pair_key_copy(step[1])):
                c.start()
        else:
            multiply(step[1], step[2:])
            send_back()
            for which, slot in sorted(k for k, v in last.items() if v == i):
                finish(which, slot)
                ready.append((which, slot))
    send_back()

    arrays = len(back_place)
    back = copy(
        results.at[pl.ds(0, arrays)], returned.at[pl.ds(0, arrays)],
        back_send, back_receive, at((0, 0, 0), 1 - core),
    )
    back.wait_recv()
    total = jnp.maximum(results[arrays], jnp.max(returned[pl.ds(0, arrays)], axis=0))
    out_ref[...] = total
    back.wait_send()
    passed, pairs = pl.ds(0, count - 1), pl.ds(0, len(shared))
    partner = at((0, 0, 0), 1 - core)
    copy(blocks.at[passed, core], blocks.at[passed, core], send, receive.at[0, 0], partner).wait_send()
    copy(keys.at[passed, core], keys.at[passed, core], key_send, receive.at[0, 0], partner).wait_send()
    copy(blocks.at[pairs, core], blocks.at[pairs, core], pair_send, receive.at[0, 0], partner).wait_send()
    copy(keys.at[pairs, core], keys.at[pairs, core], pair_key_send, receive.at[0, 0], partner).wait_send()


def body(embeddings, cluster, rank):
    count = len(OFFSETS)
    dma = pltpu.SemaphoreType.DMA
    vmem = pl.BlockSpec(memory_space=pltpu.VMEM)
    found = pl.pallas_call(
        kernel,
        out_shape=jax.ShapeDtypeStruct((1, HALF), jnp.float32),
        in_specs=[pl.BlockSpec(memory_space=pl.ANY), vmem, vmem],
        out_specs=vmem,
        scratch_shapes=[
            pltpu.VMEM((HALF, WIDTH), jnp.bfloat16),
            pltpu.VMEM((count, 2, HALF, WIDTH), jnp.bfloat16),
            pltpu.VMEM((count, 2, 1, HALF), jnp.int32),
            pltpu.VMEM((count, HALF, HALF), jnp.int32),
            pltpu.VMEM((count, HALF, HALF), jnp.float32),
            pltpu.VMEM((count, 2, 8, HALF), jnp.float32),
            pltpu.VMEM((2 * count, 1, HALF), jnp.float32),
            pltpu.VMEM((2 * count, 1, HALF), jnp.float32),
            dma(()),
            dma(()),
            dma((count, PIECES)),
            dma(()),
            dma((count,)),
            dma(()),
            dma((count,)),
            dma(()),
            dma((count,)),
            dma(()),
            dma(()),
        ],
        compiler_params=pltpu.CompilerParams(collective_id=0, has_side_effects=True),
        name="pairs",
    )(embeddings, cluster.reshape(1, HALF), rank.reshape(1, HALF))
    return found.reshape(HALF)


def solution(mesh):
    in_specs = (P(("grp", "mem"), None), P(("grp", "mem"), None), P(("grp", "mem")))
    out_specs = P(("grp", "mem"))
    return jax.shard_map(body, mesh=mesh, in_specs=in_specs, out_specs=out_specs, check_vma=False)
```

time: 37.2 us -> 34.8 us (0.935); the launches traced: 36.5 us -> 34.6 us
  Pallas kernels: 35.4 us -> 33.5 us
    pallas_call x1, Pallas kernels: 35.4 us -> 33.5 us  [body(): pl.pallas_call(kernel, out_shape=jax.ShapeDtypeStruct((1, HALF), jnp.floa...]
where the time goes in v2:
time: 34.8 us; the launch traced here: 34.6 us
  Pallas kernels  33.5 us (96%)
  local copies, waits for them, and re-layouts  1.1 us (3%)
    pallas_call x1, Pallas kernels, body(): pl.pallas_call(kernel, out_shape=jax.ShapeDtypeStruct((1, HALF), jnp.floa...  33.5 us
    unnamed x3, local copies, waits for them, and re-layouts  1.1 us

profile of v2, /device:TPU:1, one launch (start us, length us, event | category | flops | bytes accessed | tf_op | source)
XLA Modules:
  0.0 34.6 jit_solution(11569663614747761049)
XLA Ops:
  0.0 33.5 %pairs.1 = f32[1,128]{1,0:T(1,128)} custom-call(bf16[128,1024]{1,0:T(8,128)(2,1)} %x_hbm.1, s32[1,128]{1,0:T(1,128)} %bitcast.3, s32[1,128]{1,0:T(1,128)} %bitcast.4), custom_call_target="tpu_custom_call" | custom-call | tf_op jit(solution)/shard_map/pairs/pallas_call | solution.py:253
  33.5 0.0 copy-start
  33.5 0.6 %copy-done = f32[1,128]{1,0:T(1,128)S(1)} copy-done((f32[1,128]{1,0:T(1,128)S(1)}, f32[1,128]{1,0:T(1,128)}, u32[]{:S(2)}) %copy-start) | copy-done | bytes 536
  34.1 0.5 %copy.5 = f32[128]{0:T(128)} copy(f32[128]{0:T(128)S(1)} %bitcast.5) | data formatting | bytes 1024
Async XLA Ops:
  33.5 0.6 %copy-start = (f32[1,128]{1,0:T(1,128)S(1)}, f32[1,128]{1,0:T(1,128)}, u32[]{:S(2)}) copy-start(f32[1,128]{1,0:T(1,128)} %pairs.1) | copy-start | bytes 1540

commit v3 on v2

--- a/solution.py
+++ b/solution.py
@@ -7,28 +7,27 @@
 
 MESH = pl.DeviceIdType.MESH
 OFFSETS = (
-    (0, 0, 0), (0, 0, 1), (0, 0, 2), (0, 0, 3), (0, 1, 0), (0, 3, 0), (0, 3, 1),
-    (0, 3, 2), (1, 1, 0), (2, 0, 0), (2, 1, 0), (3, 0, 0), (3, 1, 0),
+    (0, 0, 0), (0, 0, 1), (0, 0, 3), (0, 1, 0), (0, 1, 1), (0, 2, 0), (0, 2, 1),
+    (0, 3, 0), (1, 0, 0), (1, 0, 3), (2, 0, 0), (2, 0, 3), (3, 0, 3),
 )
 UNITS = ((1, 0, 0), (3, 0, 0), (0, 1, 0), (0, 3, 0), (0, 0, 1), (0, 0, 3))
 PIECES = 4
 PROGRAM = (
-    ("s", 11, 3, 0, 1), ("s", 4, 1, 0, 2), ("s", 5, 0, 0, 3), ("s", 1, 1, 0, 4), ("s", 3, 2, 0, 5),
-    ("x", 0), ("s", 11, 2, 0, 1), ("s", 4, 2, 0, 2), ("s", 5, 1, 0, 3), ("s", 1, 0, 0, 4),
-    ("s", 3, 3, 0, 5), ("s", 11, 1, 0, 1), ("s", 4, 0, 0, 2), ("s", 5, 2, 0, 3), ("s", 1, 3, 0, 4),
-    ("s", 3, 0, 0, 5), ("s", 8, 1, 4, 0), ("s", 11, 0, 0, 1), ("s", 12, 3, 11, 2), ("s", 6, 1, 1, 3),
-    ("s", 1, 2, 0, 4), ("s", 2, 2, 3, 5), ("s", 8, 2, 4, 0), ("s", 9, 3, 11, 1), ("s", 12, 2, 11, 2),
-    ("s", 5, 3, 0, 3), ("s", 6, 0, 5, 4), ("s", 2, 3, 3, 5), ("s", 8, 0, 4, 0), ("s", 12, 1, 4, 1),
-    ("s", 4, 3, 0, 2), ("s", 6, 3, 1, 3), ("s", 6, 2, 5, 4), ("s", 3, 1, 0, 5), ("s", 10, 1, 8, 0),
-    ("x", 1), ("x", 11), ("s", 9, 0, 11, 1), ("s", 12, 0, 11, 2), ("s", 7, 2, 2, 3),
-    ("s", 7, 1, 6, 4), ("s", 2, 0, 3, 5), ("x", 5), ("s", 10, 0, 8, 0), ("u", 1, 0, 1, 5),
-    ("s", 10, 2, 12, 1), ("s", 10, 3, 9, 2), ("s", 7, 3, 2, 3), ("s", 7, 0, 6, 4), ("u", 11, 0, 1, 5),
-    ("s", 2, 1, 3, 5), ("x", 3), ("x", 4), ("x", 6), ("u", 1, 6, 3, 4),
-    ("u", 11, 4), ("s", 8, 3, 4, 0), ("s", 9, 1, 11, 1), ("u", 5, 4), ("x", 12),
-    ("u", 1, 12), ("u", 5, 12), ("u", 6, 3, 4, 12), ("s", 9, 2, 11, 1), ("u", 3, 12, 11),
-    ("x", 10), ("u", 4, 7, 10), ("u", 11, 7), ("u", 0, 10), ("x", 2),
-    ("u", 1, 10), ("u", 3, 10), ("u", 5, 10), ("u", 6, 10, 8), ("u", 12, 7),
-    ("u", 10, 2, 7), ("u", 11, 2), ("u", 1, 8, 9), ("u", 3, 8), ("u", 2, 8, 9),
+    ("s", 1, 2, 0, 4), ("s", 2, 1, 0, 5), ("s", 3, 0, 0, 2), ("s", 7, 0, 0, 3), ("s", 8, 1, 0, 0),
+    ("s", 1, 3, 0, 4), ("s", 2, 3, 0, 5), ("s", 3, 1, 0, 2), ("s", 7, 1, 0, 3), ("s", 8, 2, 0, 0),
+    ("s", 1, 1, 0, 4), ("s", 2, 0, 0, 5), ("s", 3, 2, 0, 2), ("s", 7, 3, 0, 3), ("s", 8, 0, 0, 0),
+    ("s", 2, 2, 0, 5), ("s", 8, 3, 0, 0), ("s", 12, 1, 2, 1), ("s", 4, 0, 3, 4), ("s", 4, 2, 1, 2),
+    ("s", 5, 0, 7, 3), ("s", 9, 1, 8, 5), ("s", 12, 3, 2, 1), ("s", 4, 1, 3, 4), ("s", 4, 3, 1, 2),
+    ("s", 5, 1, 7, 3), ("s", 10, 2, 8, 0), ("s", 1, 0, 0, 4), ("s", 9, 2, 8, 5), ("s", 12, 0, 2, 1),
+    ("s", 5, 2, 3, 2), ("s", 5, 3, 7, 3), ("s", 10, 0, 8, 0), ("s", 7, 2, 0, 3), ("s", 12, 2, 2, 1),
+    ("s", 6, 0, 5, 4), ("s", 6, 2, 4, 2), ("s", 9, 3, 8, 5), ("s", 10, 3, 8, 0), ("s", 9, 0, 8, 5),
+    ("s", 10, 1, 8, 0), ("x", 2), ("x", 8), ("s", 11, 3, 12, 1), ("s", 11, 1, 12, 1),
+    ("s", 6, 1, 5, 4), ("s", 6, 3, 4, 2), ("s", 3, 3, 0, 2), ("x", 4), ("u", 8, 4, 0, 2, 8),
+    ("s", 11, 0, 10, 5), ("s", 11, 2, 9, 0), ("x", 1), ("x", 5), ("u", 8, 5, 1),
+    ("u", 2, 1), ("u", 4, 0, 1, 2, 5), ("x", 12), ("u", 4, 12), ("x", 7),
+    ("u", 4, 7), ("x", 6), ("u", 2, 6), ("u", 8, 6, 9), ("u", 4, 9, 10),
+    ("u", 5, 10), ("u", 12, 6, 1, 5, 8, 9), ("u", 7, 9, 10, 12, 8), ("u", 1, 11), ("u", 4, 11),
+    ("u", 5, 11), ("u", 7, 11, 3), ("u", 12, 3), ("u", 8, 3), ("u", 6, 11),
 )
 HALF = 128
 WIDTH = 1024
@@ -156,13 +155,15 @@
             key_columns[slot] = jnp.broadcast_to(keys[slot, core], (HALF, HALF)).T
             columns_here.add(slot)
 
-    def multiply(b, others):
+    def need(b, others):
         for a in others:
             need_block(a)
         need_block(b)
         need_pair(b)
         for a in others:
             need_columns(a)
+
+    def multiply(b, others):
         gram = lax.dot_general(
             jnp.concatenate([blocks[a, core] for a in others], axis=0),
             blocks[b].reshape(2 * HALF, WIDTH), (((1,), (1,)), ((), ())),
@@ -207,26 +208,36 @@
                 c.start()
         ready.clear()
 
-    for i, step in enumerate(steps):
+    i = 0
+    while i < len(steps):
+        step = steps[i]
+        if step[0] == "u":
+            batch = []
+            while i < len(steps) and steps[i][0] == "u":
+                batch.append(steps[i])
+                i += 1
+            for unit in batch:
+                need(unit[1], unit[2:])
+            for unit in batch:
+                multiply(unit[1], unit[2:])
+            send_back()
+            for key in sorted(k for k, v in last.items() if i - len(batch) <= v < i):
+                finish(*key)
+                ready.append(key)
+            continue
         if step[0] == "s":
             _, slot, piece, parent, direction = step
             need_piece(parent, piece)
-            c = piece_copy(slot, piece, parent, direction)
-            c.start()
+            piece_copy(slot, piece, parent, direction).start()
             if piece == 0:
                 need_key(parent)
-                c = key_copy(slot, parent, direction)
-                c.start()
-        elif step[0] == "x":
+                key_copy(slot, parent, direction).start()
+        else:
             need_block(step[1])
-            for c in (pair_copy(step[1]), pair_key_copy(step[1])):
-                c.start()
-        else:
-            multiply(step[1], step[2:])
-            send_back()
-            for which, slot in sorted(k for k, v in last.items() if v == i):
-                finish(which, slot)
-                ready.append((which, slot))
+            pair_copy(step[1]).start()
+            pair_key_copy(step[1]).start()
+        send_back()
+        i += 1
     send_back()
 
     arrays = len(back_place)

time: 34.8 us -> 32.9 us (0.945)
  Pallas kernels: 33.5 us -> 31.7 us
    pallas_call x1, Pallas kernels: 33.5 us -> 31.7 us  [body(): pl.pallas_call(kernel, out_shape=jax.ShapeDtypeStruct((1, HALF), jnp.floa...]
where the time goes in v3:
time: 32.9 us; the launch traced here: 32.8 us
  Pallas kernels  31.7 us (96%)
  local copies, waits for them, and re-layouts  1.1 us (3%)
    pallas_call x1, Pallas kernels, body(): pl.pallas_call(kernel, out_shape=jax.ShapeDtypeStruct((1, HALF), jnp.floa...  31.7 us
    unnamed x3, local copies, waits for them, and re-layouts  1.1 us

profile of v3, /device:TPU:1, one launch (start us, length us, event | category | flops | bytes accessed | tf_op | source)
XLA Modules:
  0.0 32.8 jit_solution(3121726429029250775)
XLA Ops:
  0.0 31.7 %pairs.1 = f32[1,128]{1,0:T(1,128)} custom-call(bf16[128,1024]{1,0:T(8,128)(2,1)} %x_hbm.1, s32[1,128]{1,0:T(1,128)} %bitcast.3, s32[1,128]{1,0:T(1,128)} %bitcast.4), custom_call_target="tpu_custom_call" | custom-call | tf_op jit(solution)/shard_map/pairs/pallas_call | solution.py:264
  31.7 0.0 copy-start
  31.7 0.6 %copy-done = f32[1,128]{1,0:T(1,128)S(1)} copy-done((f32[1,128]{1,0:T(1,128)S(1)}, f32[1,128]{1,0:T(1,128)}, u32[]{:S(2)}) %copy-start) | copy-done | bytes 536
  32.3 0.5 %copy.5 = f32[128]{0:T(128)} copy(f32[128]{0:T(128)S(1)} %bitcast.5) | data formatting | bytes 1024
Async XLA Ops:
  31.7 0.6 %copy-start = (f32[1,128]{1,0:T(1,128)S(1)}, f32[1,128]{1,0:T(1,128)}, u32[]{:S(2)}) copy-start(f32[1,128]{1,0:T(1,128)} %pairs.1) | copy-start | bytes 1540

commit v4 on v3

--- a/solution.py
+++ b/solution.py
@@ -48,7 +48,7 @@
 
 
 def kernel(
-    x_hbm, cluster_ref, rank_ref, out_ref, raw, blocks, keys, key_columns, row_best, column_best,
+    x_hbm, cluster_hbm, rank_hbm, out_ref, raw, labels, label_sem, blocks, keys, key_columns, row_best, column_best,
     results, returned, raw_sem, send, receive, key_send, key_receive, pair_send, pair_receive,
     pair_key_send, pair_key_receive, back_send, back_receive,
 ):
@@ -71,9 +71,17 @@
     )
     load = pltpu.make_async_copy(x_hbm, raw, raw_sem)
     load.start()
-    keys[0, core] = cluster_ref[...] * (2 * RANKS) + rank_ref[...]
+    label_loads = [
+        pltpu.make_async_copy(source, labels.at[i], label_sem.at[i])
+        for i, source in enumerate((cluster_hbm, rank_hbm))
+    ]
+    for c in label_loads:
+        c.start()
     row_best[...] = jnp.full(row_best.shape, -1.0, jnp.float32)
     column_best[...] = jnp.full(column_best.shape, -1.0, jnp.float32)
+    for c in label_loads:
+        c.wait()
+    keys[0, core] = labels[0] * (2 * RANKS) + labels[1]
     load.wait()
     wide = raw[...].astype(jnp.float32)
     scale = lax.rsqrt(jnp.sum(wide * wide, axis=1, keepdims=True) + 1e-06)
@@ -98,26 +106,26 @@
         part = pl.ds(piece * rows, rows)
         return copy(
             blocks.at[parent, core, part], blocks.at[slot, core, part],
-            send, receive.at[slot, piece], at(back, core),
+            send, receive.at[slot - 1, piece], at(back, core),
         )
 
     def key_copy(slot, parent, direction):
         back = UNITS[direction ^ 1]
         return copy(
             keys.at[parent, core], keys.at[slot, core],
-            key_send, key_receive.at[slot], at(back, core),
+            key_send, key_receive.at[slot - 1], at(back, core),
         )
 
     def pair_copy(slot):
         return copy(
             blocks.at[slot, core], blocks.at[slot, core],
-            pair_send, pair_receive.at[slot], at((0, 0, 0), 1 - core),
+            pair_send, pair_receive.at[shared.index(slot)], at((0, 0, 0), 1 - core),
         )
 
     def pair_key_copy(slot):
         return copy(
             keys.at[slot, core], keys.at[slot, core],
-            pair_key_send, pair_key_receive.at[slot], at((0, 0, 0), 1 - core),
+            pair_key_send, pair_key_receive.at[shared.index(slot)], at((0, 0, 0), 1 - core),
         )
 
     incoming = {(s[1], s[2]): s[1:] for s in steps if s[0] == "s"}
@@ -142,11 +150,11 @@
         if slot not in pair_here:
             copy(
                 blocks.at[slot, 1 - core], blocks.at[slot, 1 - core],
-                pair_send, pair_receive.at[slot], at((0, 0, 0), 1 - core),
+                pair_send, pair_receive.at[shared.index(slot)], at((0, 0, 0), 1 - core),
             ).wait_recv()
             copy(
                 keys.at[slot, 1 - core], keys.at[slot, 1 - core],
-                pair_key_send, pair_key_receive.at[slot], at((0, 0, 0), 1 - core),
+                pair_key_send, pair_key_receive.at[shared.index(slot)], at((0, 0, 0), 1 - core),
             ).wait_recv()
             pair_here.add(slot)
 
@@ -258,16 +266,18 @@
 
 
 def body(embeddings, cluster, rank):
-    count = len(OFFSETS)
+    count, shared = len(OFFSETS), len(schedule()[1])
     dma = pltpu.SemaphoreType.DMA
     vmem = pl.BlockSpec(memory_space=pltpu.VMEM)
     found = pl.pallas_call(
         kernel,
         out_shape=jax.ShapeDtypeStruct((1, HALF), jnp.float32),
-        in_specs=[pl.BlockSpec(memory_space=pl.ANY), vmem, vmem],
+        in_specs=[pl.BlockSpec(memory_space=pl.ANY)] * 3,
         out_specs=vmem,
         scratch_shapes=[
             pltpu.VMEM((HALF, WIDTH), jnp.bfloat16),
+            pltpu.VMEM((2, 1, HALF), jnp.int32),
+            dma((2,)),
             pltpu.VMEM((count, 2, HALF, WIDTH), jnp.bfloat16),
             pltpu.VMEM((count, 2, 1, HALF), jnp.int32),
             pltpu.VMEM((count, HALF, HALF), jnp.int32),
@@ -277,13 +287,13 @@
             pltpu.VMEM((2 * count, 1, HALF), jnp.float32),
             dma(()),
             dma(()),
-            dma((count, PIECES)),
-            dma(()),
-            dma((count,)),
-            dma(()),
-            dma((count,)),
-            dma(()),
-            dma((count,)),
+            dma((count - 1, PIECES)),
+            dma(()),
+            dma((count - 1,)),
+            dma(()),
+            dma((shared,)),
+            dma(()),
+            dma((shared,)),
             dma(()),
             dma(()),
         ],

time: 32.9 us -> 32.1 us (0.976)
  Pallas kernels: 31.7 us -> 30.9 us
    pallas_call x1, Pallas kernels: 31.7 us -> 30.9 us  [body(): pl.pallas_call(kernel, out_shape=jax.ShapeDtypeStruct((1, HALF), jnp.floa...]
where the time goes in v4:
time: 32.1 us; the launch traced here: 32 us
  Pallas kernels  30.9 us (96%)
  local copies, waits for them, and re-layouts  1.1 us (3%)
    pallas_call x1, Pallas kernels, body(): pl.pallas_call(kernel, out_shape=jax.ShapeDtypeStruct((1, HALF), jnp.floa...  30.9 us
    unnamed x3, local copies, waits for them, and re-layouts  1.1 us

profile of v4, /device:TPU:1, one launch (start us, length us, event | category | flops | bytes accessed | tf_op | source)
XLA Modules:
  0.0 32.0 jit_solution(8873684334433027857)
XLA Ops:
  0.0 30.9 %pairs.1 = f32[1,128]{1,0:T(1,128)} custom-call(bf16[128,1024]{1,0:T(8,128)(2,1)} %x_hbm.1, s32[1,128]{1,0:T(1,128)} %bitcast.3, s32[1,128]{1,0:T(1,128)} %bitcast.4), custom_call_target="tpu_custom_call" | custom-call | tf_op jit(solution)/shard_map/pairs/pallas_call | solution.py:272
  30.9 0.0 copy-start
  30.9 0.6 %copy-done = f32[1,128]{1,0:T(1,128)S(1)} copy-done((f32[1,128]{1,0:T(1,128)S(1)}, f32[1,128]{1,0:T(1,128)}, u32[]{:S(2)}) %copy-start) | copy-done | bytes 536
  31.5 0.5 %copy.5 = f32[128]{0:T(128)} copy(f32[128]{0:T(128)S(1)} %bitcast.5) | data formatting | bytes 1024
Async XLA Ops:
  30.9 0.6 %copy-start = (f32[1,128]{1,0:T(1,128)S(1)}, f32[1,128]{1,0:T(1,128)}, u32[]{:S(2)}) copy-start(f32[1,128]{1,0:T(1,128)} %pairs.1) | copy-start | bytes 1540

commit v5 on v4

--- a/solution.py
+++ b/solution.py
@@ -24,10 +24,10 @@
     ("s", 10, 1, 8, 0), ("x", 2), ("x", 8), ("s", 11, 3, 12, 1), ("s", 11, 1, 12, 1),
     ("s", 6, 1, 5, 4), ("s", 6, 3, 4, 2), ("s", 3, 3, 0, 2), ("x", 4), ("u", 8, 4, 0, 2, 8),
     ("s", 11, 0, 10, 5), ("s", 11, 2, 9, 0), ("x", 1), ("x", 5), ("u", 8, 5, 1),
-    ("u", 2, 1), ("u", 4, 0, 1, 2, 5), ("x", 12), ("u", 4, 12), ("x", 7),
-    ("u", 4, 7), ("x", 6), ("u", 2, 6), ("u", 8, 6, 9), ("u", 4, 9, 10),
-    ("u", 5, 10), ("u", 12, 6, 1, 5, 8, 9), ("u", 7, 9, 10, 12, 8), ("u", 1, 11), ("u", 4, 11),
-    ("u", 5, 11), ("u", 7, 11, 3), ("u", 12, 3), ("u", 8, 3), ("u", 6, 11),
+    ("v", 2, 1), ("v", 4, 0, 1, 2, 5), ("x", 12), ("u", 4, 12), ("x", 7),
+    ("u", 4, 7), ("x", 6), ("u", 2, 6), ("v", 8, 6), ("v", 12, 6),
+    ("v", 6, 11), ("v", 1, 11), ("v", 4, 11), ("v", 5, 11), ("v", 7, 11),
+    ("u", 8, 9, 3), ("v", 4, 9, 10), ("v", 5, 10), ("v", 12, 1, 5, 8, 9, 3), ("v", 7, 9, 10, 12, 8, 3),
 )
 HALF = 128
 WIDTH = 1024
@@ -39,7 +39,7 @@
     last = {}
     shared = sorted({s[1] for s in steps if s[0] == "x"})
     for i, step in enumerate(steps):
-        if step[0] == "u":
+        if step[0] in "uv":
             for a in step[2:]:
                 last[("own", a)] = i
             for which in ("own", "other"):
@@ -221,7 +221,7 @@
         step = steps[i]
         if step[0] == "u":
             batch = []
-            while i < len(steps) and steps[i][0] == "u":
+            while i < len(steps) and steps[i][0] == ("v" if batch else "u"):
                 batch.append(steps[i])
                 i += 1
             for unit in batch:

time: 32.1 us -> 32.8 us (1.022)
  Pallas kernels: 30.9 us -> 31.5 us
    pallas_call x1, Pallas kernels: 30.9 us -> 31.5 us  [body(): pl.pallas_call(kernel, out_shape=jax.ShapeDtypeStruct((1, HALF), jnp.floa...]
where the time goes in v5:
time: 32.8 us; the launch traced here: 32.7 us
  Pallas kernels  31.5 us (96%)
  local copies, waits for them, and re-layouts  1.1 us (3%)
    pallas_call x1, Pallas kernels, body(): pl.pallas_call(kernel, out_shape=jax.ShapeDtypeStruct((1, HALF), jnp.floa...  31.5 us
    unnamed x3, local copies, waits for them, and re-layouts  1.1 us

profile of v5, /device:TPU:1, one launch (start us, length us, event | category | flops | bytes accessed | tf_op | source)
XLA Modules:
  0.0 32.7 jit_solution(13053889018661644392)
XLA Ops:
  0.0 31.5 %pairs.1 = f32[1,128]{1,0:T(1,128)} custom-call(bf16[128,1024]{1,0:T(8,128)(2,1)} %x_hbm.1, s32[1,128]{1,0:T(1,128)} %bitcast.3, s32[1,128]{1,0:T(1,128)} %bitcast.4), custom_call_target="tpu_custom_call" | custom-call | tf_op jit(solution)/shard_map/pairs/pallas_call | solution.py:272
  31.5 0.0 copy-start
  31.6 0.6 %copy-done = f32[1,128]{1,0:T(1,128)S(1)} copy-done((f32[1,128]{1,0:T(1,128)S(1)}, f32[1,128]{1,0:T(1,128)}, u32[]{:S(2)}) %copy-start) | copy-done | bytes 536
  32.1 0.5 %copy.5 = f32[128]{0:T(128)} copy(f32[128]{0:T(128)S(1)} %bitcast.5) | data formatting | bytes 1024
Async XLA Ops:
  31.5 0.6 %copy-start = (f32[1,128]{1,0:T(1,128)S(1)}, f32[1,128]{1,0:T(1,128)}, u32[]{:S(2)}) copy-start(f32[1,128]{1,0:T(1,128)} %pairs.1) | copy-start | bytes 1540
